TPU v7x, 32 devices: a whole 2x2x4 slice. The times are simulated.
32 devices in a mesh: grp: 2 (over y), tgt: 4 (over z), shot: 4 (over x, core).
Axes of the slice: x: 2, y: 2, z: 4, core: 2. Of those that a mesh axis runs over, the one named last changes fastest.
Arguments:
- adjoint_now: float32 [8, 16, 32, 256], P(('grp', 'shot'), 'tgt'), parts along dimension 0, may hold values from -6 to 6
- adjoint_later: float32 [8, 16, 32, 256], P(('grp', 'shot'), 'tgt'), parts along dimension 0, may hold values from -6 to 6
- courant: float32 [16, 32, 256], P('tgt'), may hold values from 0.15 to 0.45
- fwd_acc: bfloat16 [8, 4, 16, 32, 256], P(('grp', 'shot'), None, 'tgt'), parts along dimension 0, may hold values from -6 to 6
- surf_dest: int32 [1024, 1], P('tgt'), may hold values from 0 to 3; in each aligned block of 256 rows (0 to 255, 256 to 511, ...) at most 128 rows name the same one
- surf_cell: int32 [1024], P('tgt'), may hold values from 0 to 32767
- surf_vals: float32 [8, 4, 1024], P(('grp', 'shot'), None, 'tgt'), parts along dimension 0, may hold values from -6 to 6
Outputs:
- adjoint_final: float32 [8, 16, 32, 256], P(('grp', 'shot'), 'tgt'), parts along dimension 0
- grad: float32 [32, 32, 256], P(('grp', 'tgt')), parts along dimension 0
There are 2 independent parts, one for each index of `grp`. A program takes and returns all parts, laid end to end along the dimension named above; an argument that names none is the same for every part. Nothing has to cross between parts.
Inputs may be any that keep to these rules, and one draw needn't show every extreme that they name: `surf_dest`: in each owner's list of 256 entries at most 128 entries name one slab, a bound that some block reaches of them; every slab is named somewhere. `surf_cell`: several entries may name the same cell; their values add.
All inputs are finite; a program needn't handle non-finite values.
Results may differ from a plain program's by a relative error of at most 0.0003.
Values sent between devices are 32-bit elements; how exact they have to be, the bound alone decides.
No kernel may reach another device: no remote copies, remote signals or barrier semaphores. Data moves between devices by JAX's collectives and lax.ppermute only.
A program may use at most 128 MiB of HBM per device.

v0:
```python
import jax
import jax.numpy as jnp
from jax import lax
from jax.sharding import PartitionSpec as P

STEPS = 4
CAP = 128
COEFFS = (-205.0 / 72.0, 8.0 / 5.0, -1.0 / 5.0, 8.0 / 315.0, -1.0 / 560.0)


def with_halo(block, sides, width):
    for axis, dim in sides:
        count = lax.axis_size(axis)
        forward = [(i, i + 1) for i in range(count - 1)]
        backward = [(target, source) for source, target in forward]
        low = lax.ppermute(
            lax.slice_in_dim(block, block.shape[dim] - width, None, axis=dim), axis, forward
        )
        high = lax.ppermute(lax.slice_in_dim(block, 0, width, axis=dim), axis, backward)
        block = jnp.concatenate([low, block, high], axis=dim)
    return block


def laplace(padded):
    cells_x = padded.shape[0] - 8
    cells_y = padded.shape[1] - 8
    cells_z = padded.shape[2] - 8
    center = padded[4 : 4 + cells_x, 4 : 4 + cells_y, 4 : 4 + cells_z]
    total = 3.0 * COEFFS[0] * center
    for offset in range(1, 5):
        pairs = (
            padded[4 + offset : 4 + offset + cells_x, 4 : 4 + cells_y, 4 : 4 + cells_z]
            + padded[4 - offset : 4 - offset + cells_x, 4 : 4 + cells_y, 4 : 4 + cells_z]
        )
        pairs = (
            pairs
            + padded[4 : 4 + cells_x, 4 + offset : 4 + offset + cells_y, 4 : 4 + cells_z]
            + padded[4 : 4 + cells_x, 4 - offset : 4 - offset + cells_y, 4 : 4 + cells_z]
        )
        pairs = (
            pairs
            + padded[4 : 4 + cells_x, 4 : 4 + cells_y, 4 + offset : 4 + offset + cells_z]
            + padded[4 : 4 + cells_x, 4 : 4 + cells_y, 4 - offset : 4 - offset + cells_z]
        )
        total = total + COEFFS[offset] * pairs
    return total


def accumulate(grad_total, term):
    return grad_total + term


def inject_by_slots(surf_dest, surf_cell, surf_vals, cells):
    owners = lax.axis_size("tgt")
    target = surf_dest[:, 0]
    onehot_table = (target[:, None] == jnp.arange(owners, dtype=jnp.int32)[None, :]).astype(
        jnp.int32
    )
    ranks = jnp.sum((jnp.cumsum(onehot_table, axis=0) - 1) * onehot_table, axis=1)
    position = target * CAP + ranks
    cell_row = (
        jnp.full((owners * CAP,), -1.0, jnp.float32).at[position].set(surf_cell.astype(jnp.float32))
    )
    value_rows = jnp.zeros((STEPS, owners * CAP), jnp.float32).at[:, position].set(surf_vals[0])
    packed = jnp.concatenate([cell_row[None, :], value_rows], axis=0).reshape(
        STEPS + 1, owners, CAP
    )
    arrived = lax.all_to_all(packed, "tgt", split_axis=1, concat_axis=1, tiled=True)
    flat = arrived.reshape(STEPS + 1, owners * CAP)
    where_to = jnp.where(flat[0] >= 0.0, flat[0], float(cells)).astype(jnp.int32)
    return jnp.zeros((STEPS, cells), jnp.float32).at[:, where_to].add(flat[1:], mode="drop")


def on_device(adjoint_now, adjoint_later, courant, fwd_acc, surf_dest, surf_cell, surf_vals):
    current = adjoint_now[0]
    later_field = adjoint_later[0]
    grid_shape = current.shape
    cells = grid_shape[0] * grid_shape[1] * grid_shape[2]
    inject = inject_by_slots(surf_dest, surf_cell, surf_vals, cells)
    grad_total = jnp.zeros(grid_shape, jnp.float32)
    square = courant * courant
    for step in range(STEPS):
        padded = with_halo(current, (("tgt", 0),), 4)
        padded = jnp.pad(padded, ((0, 0), (4, 4), (4, 4)))
        fresh = (
            2.0 * current
            - later_field
            + square * laplace(padded)
            + inject[step].reshape(grid_shape)
        )
        term = fwd_acc[0, step].astype(jnp.float32) * fresh / courant
        grad_total = accumulate(grad_total, term)
        later_field = current
        current = fresh
    grad_total = lax.psum(grad_total, "shot")
    return (current[None], grad_total)


def solution(mesh):
    in_specs = (
        P(("grp", "shot"), "tgt", None, None),
        P(("grp", "shot"), "tgt", None, None),
        P("tgt", None, None),
        P(("grp", "shot"), None, "tgt", None, None),
        P("tgt", None),
        P("tgt"),
        P(("grp", "shot"), None, "tgt"),
    )
    out_specs = (P(("grp", "shot"), "tgt", None, None), P(("grp", "tgt"), None, None))
    return jax.shard_map(
        on_device, mesh=mesh, in_specs=in_specs, out_specs=out_specs, check_vma=False
    )
```

profile of v0, /device:TPU:0, one launch (start us, length us, event | category | flops | bytes accessed | tf_op | source)
XLA Modules:
  0.0 151.7 jit_solution(5388115988067436681)
XLA Ops:
  7.8 1.2 reduce-window.6
  10.8 0.8 copy.24
  11.7 1.2 scatter_custom_fusion.1
  13.7 1.4 scatter_custom_fusion
  15.7 6.3 %all-to-all-start = ((f32[5,4,128]{2,0,1:T(8,128)}), f32[5,4,128]{2,0,1:T(8,128)S(1)}, u32[]{:S(2)}, u32[]{:S(2)}) async-start(f32[5,4,128]{2,0,1:T(8,128)} %pad_maximum_fusion.8), calls=%async_computation | async-start | bytes 32768 | tf_op jit(solution)/shard_map/all_to_all | solution.py:68
  22.0 1.3 collective-permute-start
  23.3 4.6 %collective-permute-start.1 = (f32[4,32,256]{2,1,0:T(8,128)}, f32[4,32,256]{2,1,0:T(8,128)S(1)}, u32[]{:S(2)}, u32[]{:S(2)}) collective-permute-start(f32[4,32,256]{2,1,0:T(8,128)} %bitcast.55), channel_id=1, source_target_pairs={{0,4},{4,8},{8,12},{1,5},{5,9},{9,13},{2,6},{6,10},{10,14},{3,7},{... | collective-permute-start | bytes 393224 | tf_op jit(solution)/shard_map/ppermute | solution.py:16
  28.1 9.0 %scatter_custom_fusion.2 = f32[4,32768]{0,1:T(8,128)} fusion(s32[512]{0:T(512)S(1)} %bitcast.66, f32[512,4]{1,0:T(8,128)S(1)} %copy.27, f32[]{:T(128)} %constant.16.clone.1), kind=kCustom, calls=%fused_computation.7 | custom fusion | flops 2048 | bytes 524292 | tf_op jit(solution)/shard_map/scatter-add | solution.py:71
  37.1 41.4 %slice_reduce_fusion.3 = (f32[32768]{0:T(1024)S(1)}, f32[32768]{0:T(1024)S(1)}, f32[32768]{0:T(1024)S(1)}, f32[32768]{0:T(1024)S(1)}) fusion(f32[4,32768]{0,1:T(8,128)} %scatter_custom_fusion.2), kind=kLoop, calls=%fused_computation.6 | loop fusion | bytes 1048576 | tf_op jit(solution)/shard_map/slice | solution.py:89
  79.4 1.3 collective-permute-start.2
  80.7 4.6 %collective-permute-start.3 = (f32[4,32,256]{2,1,0:T(8,128)S(1)}, f32[4,32,256]{2,1,0:T(8,128)S(1)}, u32[]{:S(2)}, u32[]{:S(2)}) collective-permute-start(f32[4,32,256]{2,1,0:T(8,128)S(1)} %fusion.86), channel_id=1, source_target_pairs={{0,4},{4,8},{8,12},{1,5},{5,9},{9,13},{2,6},{6,10},{10,14},{3,7},{... | collective-permute-start | bytes 393224 | tf_op jit(solution)/shard_map/ppermute | solution.py:16
  85.3 1.0 collective-permute-done.2
  86.3 1.5 collective-permute-done.3
  88.6 1.3 collective-permute-start.4
  89.9 5.0 %collective-permute-start.5 = (f32[4,32,256]{2,1,0:T(8,128)S(1)}, f32[4,32,256]{2,1,0:T(8,128)S(1)}, u32[]{:S(2)}, u32[]{:S(2)}) collective-permute-start(f32[4,32,256]{2,1,0:T(8,128)S(1)} %fusion.63), channel_id=1, source_target_pairs={{0,4},{4,8},{8,12},{1,5},{5,9},{9,13},{2,6},{6,10},{10,14},{3,7},{... | collective-permute-start | bytes 393224 | tf_op jit(solution)/shard_map/ppermute | solution.py:16
  95.0 1.0 collective-permute-done.4
  95.9 1.5 collective-permute-done.5
  98.3 1.3 collective-permute-start.6
  99.6 5.0 %collective-permute-start.7 = (f32[4,32,256]{2,1,0:T(8,128)S(1)}, f32[4,32,256]{2,1,0:T(8,128)S(1)}, u32[]{:S(2)}, u32[]{:S(2)}) collective-permute-start(f32[4,32,256]{2,1,0:T(8,128)S(1)} %fusion.40), channel_id=1, source_target_pairs={{0,4},{4,8},{8,12},{1,5},{5,9},{9,13},{2,6},{6,10},{10,14},{3,7},{... | collective-permute-start | bytes 393224 | tf_op jit(solution)/shard_map/ppermute | solution.py:16
  104.6 1.0 collective-permute-done.6
  105.6 1.5 collective-permute-done.7
  107.4 1.3 fusion.110
  108.7 34.6 %all-reduce.6.cloned.1.call-done = f32[4,32,256]{2,1,0:T(8,128)} async-done(((f32[4,32,256]{2,1,0:T(8,128)}), f32[4,32,256]{2,1,0:T(8,128)}) %all-reduce.6.cloned.1.call-update) | async-done | bytes 131088 | tf_op jit(solution)/shard_map/psum | solution.py:95
  143.3 1.6 %copy.31 = f32[4,32,256]{2,1,0:T(8,128)} copy(f32[4,32,256]{2,1,0:T(8,128)} %all-reduce.6.cloned.1.call-done) | data formatting | bytes 262144
  (39 shorter events, 7.1 us)
Async XLA Ops:
  15.7 12.2 %all-to-all-start = ((f32[5,4,128]{2,0,1:T(8,128)}), f32[5,4,128]{2,0,1:T(8,128)S(1)}, u32[]{:S(2)}, u32[]{:S(2)}) async-start(f32[5,4,128]{2,0,1:T(8,128)} %pad_maximum_fusion.8), calls=%async_computation | async-start | bytes 32768 | tf_op jit(solution)/shard_map/all_to_all | solution.py:68
  22.0 121.2 %all-reduce.6.cloned.1.call-start = ((), (), s32[]{:S(2)}) async-start(), calls=%async_computation.1 | async-start | bytes 262144 | tf_op jit(solution)/shard_map/psum | solution.py:95
  22.0 56.5 %collective-permute-start = (f32[4,32,256]{2,1,0:T(8,128)}, f32[4,32,256]{2,1,0:T(8,128)S(1)}, u32[]{:S(2)}, u32[]{:S(2)}) collective-permute-start(f32[4,32,256]{2,1,0:T(8,128)} %bitcast.54), channel_id=1, source_target_pairs={{4,0},{8,4},{12,8},{5,1},{9,5},{13,9},{6,2},{10,6},{14,10},{7,3},{... | collective-permute-start | bytes 393224 | tf_op jit(solution)/shard_map/ppermute | solution.py:19
  23.3 55.2 %collective-permute-start.1 = (f32[4,32,256]{2,1,0:T(8,128)}, f32[4,32,256]{2,1,0:T(8,128)S(1)}, u32[]{:S(2)}, u32[]{:S(2)}) collective-permute-start(f32[4,32,256]{2,1,0:T(8,128)} %bitcast.55), channel_id=1, source_target_pairs={{0,4},{4,8},{8,12},{1,5},{5,9},{9,13},{2,6},{6,10},{10,14},{3,7},{... | collective-permute-start | bytes 393224 | tf_op jit(solution)/shard_map/ppermute | solution.py:16
  37.1 41.5 %copy-start.1 = (f32[1,4,32,256]{3,2,1,0:T(8,128)S(1)}, f32[1,4,32,256]{3,2,1,0:T(8,128)}, u32[]{:S(2)}) copy-start(f32[1,4,32,256]{3,2,1,0:T(8,128)} %param.7) | copy-start | bytes 393220
  37.1 41.7 %copy-start = (f32[4,32,256]{2,1,0:T(8,128)S(1)}, f32[4,32,256]{2,1,0:T(8,128)}, u32[]{:S(2)}) copy-start(f32[4,32,256]{2,1,0:T(8,128)} %param.9) | copy-start | bytes 393220
  37.1 41.7 %copy-start.3 = (f32[1,4,32,256]{3,2,1,0:T(8,128)S(1)}, f32[1,4,32,256]{3,2,1,0:T(8,128)}, u32[]{:S(2)}) copy-start(f32[1,4,32,256]{3,2,1,0:T(8,128)} %param.8) | copy-start | bytes 393220
  37.1 70.3 %copy-start.2 = (bf16[1,4,4,32,256]{4,3,2,1,0:T(8,128)(2,1)S(1)}, bf16[1,4,4,32,256]{4,3,2,1,0:T(8,128)(2,1)}, u32[]{:S(2)}) copy-start(bf16[1,4,4,32,256]{4,3,2,1,0:T(8,128)(2,1)} %param.10) | copy-start | bytes 786436
  79.4 6.9 %collective-permute-start.2 = (f32[4,32,256]{2,1,0:T(8,128)S(1)}, f32[4,32,256]{2,1,0:T(8,128)S(1)}, u32[]{:S(2)}, u32[]{:S(2)}) collective-permute-start(f32[4,32,256]{2,1,0:T(8,128)S(1)} %fusion.86), channel_id=1, source_target_pairs={{4,0},{8,4},{12,8},{5,1},{9,5},{13,9},{6,2},{10,6},{14,10},{7,3},{... | collective-permute-start | bytes 393224 | tf_op jit(solution)/shard_map/ppermute | solution.py:19
  80.7 7.1 %collective-permute-start.3 = (f32[4,32,256]{2,1,0:T(8,128)S(1)}, f32[4,32,256]{2,1,0:T(8,128)S(1)}, u32[]{:S(2)}, u32[]{:S(2)}) collective-permute-start(f32[4,32,256]{2,1,0:T(8,128)S(1)} %fusion.86), channel_id=1, source_target_pairs={{0,4},{4,8},{8,12},{1,5},{5,9},{9,13},{2,6},{6,10},{10,14},{3,7},{... | collective-permute-start | bytes 393224 | tf_op jit(solution)/shard_map/ppermute | solution.py:16
  88.6 7.3 %collective-permute-start.4 = (f32[4,32,256]{2,1,0:T(8,128)S(1)}, f32[4,32,256]{2,1,0:T(8,128)S(1)}, u32[]{:S(2)}, u32[]{:S(2)}) collective-permute-start(f32[4,32,256]{2,1,0:T(8,128)S(1)} %fusion.63), channel_id=1, source_target_pairs={{4,0},{8,4},{12,8},{5,1},{9,5},{13,9},{6,2},{10,6},{14,10},{7,3},{... | collective-permute-start | bytes 393224 | tf_op jit(solution)/shard_map/ppermute | solution.py:19
  89.9 7.5 %collective-permute-start.5 = (f32[4,32,256]{2,1,0:T(8,128)S(1)}, f32[4,32,256]{2,1,0:T(8,128)S(1)}, u32[]{:S(2)}, u32[]{:S(2)}) collective-permute-start(f32[4,32,256]{2,1,0:T(8,128)S(1)} %fusion.63), channel_id=1, source_target_pairs={{0,4},{4,8},{8,12},{1,5},{5,9},{9,13},{2,6},{6,10},{10,14},{3,7},{... | collective-permute-start | bytes 393224 | tf_op jit(solution)/shard_map/ppermute | solution.py:16
  98.3 7.3 %collective-permute-start.6 = (f32[4,32,256]{2,1,0:T(8,128)S(1)}, f32[4,32,256]{2,1,0:T(8,128)S(1)}, u32[]{:S(2)}, u32[]{:S(2)}) collective-permute-start(f32[4,32,256]{2,1,0:T(8,128)S(1)} %fusion.40), channel_id=1, source_target_pairs={{4,0},{8,4},{12,8},{5,1},{9,5},{13,9},{6,2},{10,6},{14,10},{7,3},{... | collective-permute-start | bytes 393224 | tf_op jit(solution)/shard_map/ppermute | solution.py:19
  99.6 7.5 %collective-permute-start.7 = (f32[4,32,256]{2,1,0:T(8,128)S(1)}, f32[4,32,256]{2,1,0:T(8,128)S(1)}, u32[]{:S(2)}, u32[]{:S(2)}) collective-permute-start(f32[4,32,256]{2,1,0:T(8,128)S(1)} %fusion.40), channel_id=1, source_target_pairs={{0,4},{4,8},{8,12},{1,5},{5,9},{9,13},{2,6},{6,10},{10,14},{3,7},{... | collective-permute-start | bytes 393224 | tf_op jit(solution)/shard_map/ppermute | solution.py:16
Sparse Core Ops, SparseCore 0:
  108.8 34.3 all-reduce.5
where the time goes:
time: 152 us
  local copies, waits for them, and re-layouts  47.1 us (31%)
  waiting for transfers between devices  41.9 us (28%)
  starting transfers between devices  30.6 us (20%)
  other arithmetic  17.8 us (12%)
  between operations  14.3 us (9%)
    slice x1, local copies, waits for them, and re-layouts, on_device(): inject[step].reshape(grid_shape)  41.4 us
    psum x1, waiting for transfers between devices, on_device(): grad_total = lax.psum(grad_total, 'shot')  34.6 us
    ppermute x4, starting transfers between devices, with_halo(): lax.ppermute(lax.slice_in_dim(block, block.shape[dim] - width, None, axis...  19.1 us
    scatter-add x1, other arithmetic, inject_by_slots(): jnp.zeros((STEPS, cells), jnp.float32).at[:, where_to]  8.99 us
    all_to_all x1, starting transfers between devices, inject_by_slots(): lax.all_to_all(packed, 'tgt', split_axis=1, concat_axis=1, tiled=True)  6.32 us
    ppermute x4, starting transfers between devices, with_halo(): lax.ppermute(lax.slice_in_dim(block, 0, width, axis=dim), axis, backward)  5.16 us
    ppermute x4, waiting for transfers between devices, with_halo(): lax.ppermute(lax.slice_in_dim(block, block.shape[dim] - width, None, axis...  4.49 us
  transfers between devices with their start and end apart: 10, of which 7 were waited for; matrix products, arithmetic and copies ran while one was open for 33% of the time, Pallas kernels for 0%

commit v1 on v0

--- a/solution.py
+++ b/solution.py
@@ -65,7 +65,10 @@
     packed = jnp.concatenate([cell_row[None, :], value_rows], axis=0).reshape(
         STEPS + 1, owners, CAP
     )
-    arrived = lax.all_to_all(packed, "tgt", split_axis=1, concat_axis=1, tiled=True)
+    arrived = jnp.concatenate(
+        lax.all_to_all(jnp.stack(jnp.split(packed, lax.axis_size("tgt"), axis=1)), "tgt", 0, 0),
+        axis=1,
+    )
     flat = arrived.reshape(STEPS + 1, owners * CAP)
     where_to = jnp.where(flat[0] >= 0.0, flat[0], float(cells)).astype(jnp.int32)
     return jnp.zeros((STEPS, cells), jnp.float32).at[:, where_to].add(flat[1:], mode="drop")

time: 152 us -> 152 us (level)
  no operation moved by 1% of the time
where the time goes in v1:
time: 152 us
  local copies, waits for them, and re-layouts  47.1 us (31%)
  waiting for transfers between devices  41.9 us (28%)
  starting transfers between devices  30.6 us (20%)
  other arithmetic  17.8 us (12%)
  between operations  14.3 us (9%)
    slice x1, local copies, waits for them, and re-layouts, on_device(): inject[step].reshape(grid_shape)  41.4 us
    psum x1, waiting for transfers between devices, on_device(): grad_total = lax.psum(grad_total, 'shot')  34.6 us
    ppermute x4, starting transfers between devices, with_halo(): lax.ppermute(lax.slice_in_dim(block, block.shape[dim] - width, None, axis...  19.1 us
    scatter-add x1, other arithmetic, inject_by_slots(): jnp.zeros((STEPS, cells), jnp.float32).at[:, where_to]  8.99 us
    all_to_all x1, starting transfers between devices, inject_by_slots(): lax.all_to_all(jnp.stack(jnp.split(packed, lax.axis_size('tgt'), axis=1))...  6.32 us
    ppermute x4, starting transfers between devices, with_halo(): lax.ppermute(lax.slice_in_dim(block, 0, width, axis=dim), axis, backward)  5.16 us
    ppermute x4, waiting for transfers between devices, with_halo(): lax.ppermute(lax.slice_in_dim(block, block.shape[dim] - width, None, axis...  4.49 us
  transfers between devices with their start and end apart: 10, of which 7 were waited for; matrix products, arithmetic and copies ran while one was open for 33% of the time, Pallas kernels for 0%

profile of v1, /device:TPU:0, one launch (start us, length us, event | category | flops | bytes accessed | tf_op | source)
XLA Modules:
  0.0 151.7 jit_solution(13786091490973836141)
XLA Ops:
  7.8 1.2 reduce-window.6
  10.8 0.8 copy.26
  11.7 1.2 scatter_custom_fusion.1
  13.7 1.4 scatter_custom_fusion
  15.7 6.3 %all-to-all-start = ((f32[4,5,1,128]{3,2,1,0:T(1,128)}), f32[4,5,1,128]{3,2,1,0:T(1,128)S(1)}, u32[]{:S(2)}, u32[]{:S(2)}) async-start(f32[4,5,1,128]{3,2,1,0:T(1,128)} %pad_maximum_fusion.8), calls=%async_computation | async-start | bytes 20480 | tf_op jit(solution)/shard_map/all_to_all | solution.py:69
  22.0 1.3 collective-permute-start
  23.3 4.6 %collective-permute-start.1 = (f32[4,32,256]{2,1,0:T(8,128)}, f32[4,32,256]{2,1,0:T(8,128)S(1)}, u32[]{:S(2)}, u32[]{:S(2)}) collective-permute-start(f32[4,32,256]{2,1,0:T(8,128)} %bitcast.61), channel_id=1, source_target_pairs={{0,4},{4,8},{8,12},{1,5},{5,9},{9,13},{2,6},{6,10},{10,14},{3,7},{... | collective-permute-start | bytes 393224 | tf_op jit(solution)/shard_map/ppermute | solution.py:16
  28.1 9.0 %scatter_custom_fusion.2 = f32[4,32768]{0,1:T(8,128)} fusion(s32[512]{0:T(512)S(1)} %bitcast.75, f32[512,4]{1,0:T(8,128)S(1)} %copy.29, f32[]{:T(128)} %constant.16.clone.1), kind=kCustom, calls=%fused_computation.7 | custom fusion | flops 2048 | bytes 524292 | tf_op jit(solution)/shard_map/scatter-add | solution.py:74
  37.1 41.4 %slice_reduce_fusion.3 = (f32[32768]{0:T(1024)S(1)}, f32[32768]{0:T(1024)S(1)}, f32[32768]{0:T(1024)S(1)}, f32[32768]{0:T(1024)S(1)}) fusion(f32[4,32768]{0,1:T(8,128)} %scatter_custom_fusion.2), kind=kLoop, calls=%fused_computation.6 | loop fusion | bytes 1048576 | tf_op jit(solution)/shard_map/slice | solution.py:92
  79.4 1.3 collective-permute-start.2
  80.7 4.6 %collective-permute-start.3 = (f32[4,32,256]{2,1,0:T(8,128)S(1)}, f32[4,32,256]{2,1,0:T(8,128)S(1)}, u32[]{:S(2)}, u32[]{:S(2)}) collective-permute-start(f32[4,32,256]{2,1,0:T(8,128)S(1)} %fusion.86), channel_id=1, source_target_pairs={{0,4},{4,8},{8,12},{1,5},{5,9},{9,13},{2,6},{6,10},{10,14},{3,7},{... | collective-permute-start | bytes 393224 | tf_op jit(solution)/shard_map/ppermute | solution.py:16
  85.3 1.0 collective-permute-done.2
  86.3 1.5 collective-permute-done.3
  88.7 1.3 collective-permute-start.4
  90.0 5.0 %collective-permute-start.5 = (f32[4,32,256]{2,1,0:T(8,128)S(1)}, f32[4,32,256]{2,1,0:T(8,128)S(1)}, u32[]{:S(2)}, u32[]{:S(2)}) collective-permute-start(f32[4,32,256]{2,1,0:T(8,128)S(1)} %fusion.63), channel_id=1, source_target_pairs={{0,4},{4,8},{8,12},{1,5},{5,9},{9,13},{2,6},{6,10},{10,14},{3,7},{... | collective-permute-start | bytes 393224 | tf_op jit(solution)/shard_map/ppermute | solution.py:16
  95.0 1.0 collective-permute-done.4
  96.0 1.5 collective-permute-done.5
  98.3 1.3 collective-permute-start.6
  99.6 5.0 %collective-permute-start.7 = (f32[4,32,256]{2,1,0:T(8,128)S(1)}, f32[4,32,256]{2,1,0:T(8,128)S(1)}, u32[]{:S(2)}, u32[]{:S(2)}) collective-permute-start(f32[4,32,256]{2,1,0:T(8,128)S(1)} %fusion.40), channel_id=1, source_target_pairs={{0,4},{4,8},{8,12},{1,5},{5,9},{9,13},{2,6},{6,10},{10,14},{3,7},{... | collective-permute-start | bytes 393224 | tf_op jit(solution)/shard_map/ppermute | solution.py:16
  104.7 1.0 collective-permute-done.6
  105.6 1.5 collective-permute-done.7
  107.4 1.3 fusion.110
  108.7 34.6 %all-reduce.6.cloned.1.call-done = f32[4,32,256]{2,1,0:T(8,128)} async-done(((f32[4,32,256]{2,1,0:T(8,128)}), f32[4,32,256]{2,1,0:T(8,128)}) %all-reduce.6.cloned.1.call-update) | async-done | bytes 131088 | tf_op jit(solution)/shard_map/psum | solution.py:98
  143.3 1.6 %copy.33 = f32[4,32,256]{2,1,0:T(8,128)} copy(f32[4,32,256]{2,1,0:T(8,128)} %all-reduce.6.cloned.1.call-done) | data formatting | bytes 262144
  (40 shorter events, 7.1 us)
Async XLA Ops:
  15.7 12.2 %all-to-all-start = ((f32[4,5,1,128]{3,2,1,0:T(1,128)}), f32[4,5,1,128]{3,2,1,0:T(1,128)S(1)}, u32[]{:S(2)}, u32[]{:S(2)}) async-start(f32[4,5,1,128]{3,2,1,0:T(1,128)} %pad_maximum_fusion.8), calls=%async_computation | async-start | bytes 20480 | tf_op jit(solution)/shard_map/all_to_all | solution.py:69
  22.0 121.2 %all-reduce.6.cloned.1.call-start = ((), (), s32[]{:S(2)}) async-start(), calls=%async_computation.1 | async-start | bytes 262144 | tf_op jit(solution)/shard_map/psum | solution.py:98
  22.0 56.5 %collective-permute-start = (f32[4,32,256]{2,1,0:T(8,128)}, f32[4,32,256]{2,1,0:T(8,128)S(1)}, u32[]{:S(2)}, u32[]{:S(2)}) collective-permute-start(f32[4,32,256]{2,1,0:T(8,128)} %bitcast.60), channel_id=1, source_target_pairs={{4,0},{8,4},{12,8},{5,1},{9,5},{13,9},{6,2},{10,6},{14,10},{7,3},{... | collective-permute-start | bytes 393224 | tf_op jit(solution)/shard_map/ppermute | solution.py:19
  23.3 55.2 %collective-permute-start.1 = (f32[4,32,256]{2,1,0:T(8,128)}, f32[4,32,256]{2,1,0:T(8,128)S(1)}, u32[]{:S(2)}, u32[]{:S(2)}) collective-permute-start(f32[4,32,256]{2,1,0:T(8,128)} %bitcast.61), channel_id=1, source_target_pairs={{0,4},{4,8},{8,12},{1,5},{5,9},{9,13},{2,6},{6,10},{10,14},{3,7},{... | collective-permute-start | bytes 393224 | tf_op jit(solution)/shard_map/ppermute | solution.py:16
  37.1 41.5 %copy-start.1 = (f32[1,4,32,256]{3,2,1,0:T(8,128)S(1)}, f32[1,4,32,256]{3,2,1,0:T(8,128)}, u32[]{:S(2)}) copy-start(f32[1,4,32,256]{3,2,1,0:T(8,128)} %param.7) | copy-start | bytes 393220
  37.1 41.7 %copy-start = (f32[4,32,256]{2,1,0:T(8,128)S(1)}, f32[4,32,256]{2,1,0:T(8,128)}, u32[]{:S(2)}) copy-start(f32[4,32,256]{2,1,0:T(8,128)} %param.9) | copy-start | bytes 393220
  37.1 41.7 %copy-start.3 = (f32[1,4,32,256]{3,2,1,0:T(8,128)S(1)}, f32[1,4,32,256]{3,2,1,0:T(8,128)}, u32[]{:S(2)}) copy-start(f32[1,4,32,256]{3,2,1,0:T(8,128)} %param.8) | copy-start | bytes 393220
  37.1 70.3 %copy-start.2 = (bf16[1,4,4,32,256]{4,3,2,1,0:T(8,128)(2,1)S(1)}, bf16[1,4,4,32,256]{4,3,2,1,0:T(8,128)(2,1)}, u32[]{:S(2)}) copy-start(bf16[1,4,4,32,256]{4,3,2,1,0:T(8,128)(2,1)} %param.10) | copy-start | bytes 786436
  79.4 6.9 %collective-permute-start.2 = (f32[4,32,256]{2,1,0:T(8,128)S(1)}, f32[4,32,256]{2,1,0:T(8,128)S(1)}, u32[]{:S(2)}, u32[]{:S(2)}) collective-permute-start(f32[4,32,256]{2,1,0:T(8,128)S(1)} %fusion.86), channel_id=1, source_target_pairs={{4,0},{8,4},{12,8},{5,1},{9,5},{13,9},{6,2},{10,6},{14,10},{7,3},{... | collective-permute-start | bytes 393224 | tf_op jit(solution)/shard_map/ppermute | solution.py:19
  80.7 7.1 %collective-permute-start.3 = (f32[4,32,256]{2,1,0:T(8,128)S(1)}, f32[4,32,256]{2,1,0:T(8,128)S(1)}, u32[]{:S(2)}, u32[]{:S(2)}) collective-permute-start(f32[4,32,256]{2,1,0:T(8,128)S(1)} %fusion.86), channel_id=1, source_target_pairs={{0,4},{4,8},{8,12},{1,5},{5,9},{9,13},{2,6},{6,10},{10,14},{3,7},{... | collective-permute-start | bytes 393224 | tf_op jit(solution)/shard_map/ppermute | solution.py:16
  88.7 7.3 %collective-permute-start.4 = (f32[4,32,256]{2,1,0:T(8,128)S(1)}, f32[4,32,256]{2,1,0:T(8,128)S(1)}, u32[]{:S(2)}, u32[]{:S(2)}) collective-permute-start(f32[4,32,256]{2,1,0:T(8,128)S(1)} %fusion.63), channel_id=1, source_target_pairs={{4,0},{8,4},{12,8},{5,1},{9,5},{13,9},{6,2},{10,6},{14,10},{7,3},{... | collective-permute-start | bytes 393224 | tf_op jit(solution)/shard_map/ppermute | solution.py:19
  90.0 7.5 %collective-permute-start.5 = (f32[4,32,256]{2,1,0:T(8,128)S(1)}, f32[4,32,256]{2,1,0:T(8,128)S(1)}, u32[]{:S(2)}, u32[]{:S(2)}) collective-permute-start(f32[4,32,256]{2,1,0:T(8,128)S(1)} %fusion.63), channel_id=1, source_target_pairs={{0,4},{4,8},{8,12},{1,5},{5,9},{9,13},{2,6},{6,10},{10,14},{3,7},{... | collective-permute-start | bytes 393224 | tf_op jit(solution)/shard_map/ppermute | solution.py:16
  98.3 7.3 %collective-permute-start.6 = (f32[4,32,256]{2,1,0:T(8,128)S(1)}, f32[4,32,256]{2,1,0:T(8,128)S(1)}, u32[]{:S(2)}, u32[]{:S(2)}) collective-permute-start(f32[4,32,256]{2,1,0:T(8,128)S(1)} %fusion.40), channel_id=1, source_target_pairs={{4,0},{8,4},{12,8},{5,1},{9,5},{13,9},{6,2},{10,6},{14,10},{7,3},{... | collective-permute-start | bytes 393224 | tf_op jit(solution)/shard_map/ppermute | solution.py:19
  99.6 7.5 %collective-permute-start.7 = (f32[4,32,256]{2,1,0:T(8,128)S(1)}, f32[4,32,256]{2,1,0:T(8,128)S(1)}, u32[]{:S(2)}, u32[]{:S(2)}) collective-permute-start(f32[4,32,256]{2,1,0:T(8,128)S(1)} %fusion.40), channel_id=1, source_target_pairs={{0,4},{4,8},{8,12},{1,5},{5,9},{9,13},{2,6},{6,10},{10,14},{3,7},{... | collective-permute-start | bytes 393224 | tf_op jit(solution)/shard_map/ppermute | solution.py:16
Sparse Core Ops, SparseCore 0:
  108.8 34.3 all-reduce.5
